TPU v7x, 128 devices: a whole 4x4x4 slice. The times are simulated.
128 devices in a mesh: rows: 16 (over x, z), cols: 8 (over y, core).
Axes of the slice: x: 4, y: 4, z: 4, core: 2. Of those that a mesh axis runs over, the one named last changes fastest.
Arguments:
- band: float32 [16, 8, 1024, 1024], P('rows', 'cols'), may hold values from -6 to 6
- diag: float32 [8, 1024, 1024], P('cols', 'rows'), as said below
- row_factors: bfloat16 [16, 8, 2, 1024, 256], P('rows', 'cols'), as said below
- row_ranks: int32 [16, 8], P('rows', 'cols'), may hold values from 32 to 256
- col_factors: bfloat16 [8, 8, 2, 1024, 256], P(None, 'cols', None, 'rows'), as said below
- col_ranks: int32 [8, 8], replicated, may hold values from 32 to 256
Outputs:
- band_out: float32 [16, 8, 1024, 1024], P('rows', 'cols')
- diag_out: float32 [8, 1024, 1024], P('cols', 'rows')
Inputs may be any that keep to these rules, and one draw needn't show every extreme that they name: `diag`: every new_diag[c] is symmetric positive definite. `row_factors`: columns of a factor beyond its rank hold arbitrary values. `col_factors`: columns of a factor beyond its rank hold arbitrary values.
All inputs are finite; a program needn't handle non-finite values.
Results may differ from a plain program's by a relative error of at most 0.002.
Values may be sent and summed in bfloat16 or wider, within the bound.
No kernel may reach another device: no remote copies, remote signals or barrier semaphores. Data moves between devices by JAX's collectives and lax.ppermute only.
A program may use at most 128 MiB of HBM per device.

v0:
```python
import jax
import jax.numpy as jnp
from jax import lax
from jax.sharding import PartitionSpec as P


def core_of(side_row, rank_row, side_col, rank_col):
    pair_core = lax.dot_general(
        side_row, side_col, (((0,), (0,)), ((), ())), preferred_element_type=jnp.float32
    )
    row_positions = jnp.arange(side_row.shape[1], dtype=jnp.int32)
    col_positions = jnp.arange(side_col.shape[1], dtype=jnp.int32)
    kept_mask = (row_positions[:, None] < rank_row) & (col_positions[None, :] < rank_col)
    return jnp.where(kept_mask, pair_core, 0.0).astype(jnp.bfloat16)


def weighted(base_row, side_row, rank_row, side_col, rank_col):
    pair_core = core_of(side_row, rank_row, side_col, rank_col)
    return jnp.dot(base_row, pair_core, preferred_element_type=jnp.float32).astype(jnp.bfloat16)


def finish(left_part, base_col):
    return lax.dot_general(
        left_part, base_col, (((1,), (1,)), ((), ())), preferred_element_type=jnp.float32
    )


def pair_weighted(base_row, side_row, rank_row, side_col, rank_col):
    return weighted(base_row, side_row, rank_row, side_col, rank_col)


def pair_tile(base_row, side_row, rank_row, base_col, side_col, rank_col):
    return finish(weighted(base_row, side_row, rank_row, side_col, rank_col), base_col)


def shards(band, diag, row_factors, row_ranks, col_factors, col_ranks):
    column = lax.axis_index("cols")
    slab_idx = lax.axis_index("rows")
    row_count = row_factors.shape[0]
    slab_rows = diag.shape[1]
    tile_order = band.shape[-1]
    own_ranks = lax.dynamic_index_in_dim(col_ranks, column, 0, keepdims=False)
    own_column = lax.all_to_all(col_factors, "cols", split_axis=0, concat_axis=1, tiled=True)
    full_column = lax.all_gather(own_column, "rows", axis=3, tiled=True)
    base_full = full_column[0, :, 0]
    side_full = full_column[0, :, 1]
    base_slab = own_column[0, :, 0]
    start_sum = jnp.zeros((row_count, tile_order, tile_order), jnp.float32)
    factors = lax.all_gather(row_factors, "cols", axis=1, tiled=True)
    piece_ranks = lax.all_gather(row_ranks, "cols", axis=1, tiled=True)

    def advance(inner, carried):
        base_col = lax.dynamic_index_in_dim(base_full, inner, 0, keepdims=False)
        side_col = lax.dynamic_index_in_dim(side_full, inner, 0, keepdims=False)
        rank_col = lax.dynamic_index_in_dim(own_ranks, inner, 0, keepdims=False)
        row_part = lax.dynamic_index_in_dim(factors, inner, 1, keepdims=False)
        row_rank = lax.dynamic_index_in_dim(piece_ranks, inner, 1, keepdims=False)
        tile_terms = [
            pair_tile(row_part[0, 0], row_part[0, 1], row_rank[0], base_col, side_col, rank_col)
        ]
        return carried + jnp.stack(tile_terms)

    update = lax.fori_loop(0, factors.shape[1], advance, start_sum)

    def diag_left(panel_idx):
        side_col = lax.dynamic_index_in_dim(side_full, panel_idx, 0, keepdims=False)
        base_row = lax.dynamic_index_in_dim(base_slab, panel_idx, 0, keepdims=False)
        rank_col = lax.dynamic_index_in_dim(own_ranks, panel_idx, 0, keepdims=False)
        return pair_weighted(base_row, side_col, rank_col, side_col, rank_col)

    diag_parts = lax.map(diag_left, jnp.arange(base_full.shape[0], dtype=jnp.int32))
    diag_term = jnp.einsum("kxr,kyr->xy", diag_parts, base_full, preferred_element_type=jnp.float32)
    updated = band[:, 0] - update
    new_slab = diag[0] - diag_term
    whole_diag = lax.all_gather(new_slab, "rows", axis=0, tiled=True)
    factor = jnp.linalg.cholesky(whole_diag)
    stacked = updated.reshape(row_count * tile_order, tile_order)
    solved = jax.scipy.linalg.solve_triangular(factor, stacked.T, lower=True).T.reshape(
        row_count, tile_order, tile_order
    )
    is_first = column == 0
    band_out = jnp.where(is_first, solved, updated)[:, None]
    factor_slab = lax.dynamic_slice_in_dim(factor, slab_idx * slab_rows, slab_rows, 0)
    diag_out = jnp.where(is_first, factor_slab, new_slab)[None]
    return (band_out, diag_out)


def solution(mesh):
    placed = (
        P("rows", "cols", None, None),
        P("cols", "rows", None),
        P("rows", "cols", None, None, None),
        P("rows", "cols"),
        P(None, "cols", None, "rows", None),
        P(),
    )
    return jax.shard_map(
        shards,
        mesh=mesh,
        in_specs=placed,
        out_specs=(P("rows", "cols", None, None), P("cols", "rows", None)),
        check_vma=False,
    )
```

profile of v0, /device:TPU:1, one launch (start us, length us, event | category | flops | bytes accessed | tf_op | source)
XLA Modules:
  0.0 612.0 jit_solution(13151042446504265048)
XLA Ops:
  7.2 15.3 %all_to_all.12 = bf16[8,1,2,64,256]{4,3,2,1,0:T(8,128)(2,1)S(1)} all-to-all(bf16[8,1,2,64,256]{4,3,2,1,0:T(8,128)(2,1)} %param.14), channel_id=1, replica_groups=mesh['rows'=16,'cols'=8] {'cols'}, dimensions={0} | all-to-all | bytes 1048576 | tf_op jit(solution)/shard_map/all_to_all | solution.py:43
  26.7 6.5 %all-reduce.1 = s32[8]{0:T(128)S(1)} all-reduce(s32[8]{0:T(128)S(1)} %bitcast_dynamic-update-slice_fusion.1), channel_id=1, replica_groups=mesh['rows'=16,'cols'=8] {'cols'}, use_global_device_ids=true, to_apply=%add.1 | all-reduce | flops 8 | bytes 64
  33.2 5.5 copy.34
  38.8 56.3 %all-gather.9.cloned.1.call-done = bf16[8,1,2,1024,256]{4,3,0,2,1:T(8,128)(2,1)} async-done(((bf16[8,1,2,64,256]{4,3,0,2,1:T(8,128)(2,1)}), bf16[8,1,2,1024,256]{4,3,0,2,1:T(8,128)(2,1)}) %all-gather.9.cloned.1.call-update) | async-done | bytes 8388624 | tf_op jit(solution)/shard_map/all_gather | solution.py:44
  95.0 5.8 slice_bitcast_fusion.5
  100.8 46.8 %while.25 = (s32[]{:T(128)}, bf16[8,64,256]{2,1,0:T(8,128)(2,1)S(1)}, s32[8]{0:T(128)S(1)}, bf16[8,64,256]{2,1,0:T(8,128)(2,1)S(1)}, s32[8]{0:T(128)S(1)}, /*ind...) while((s32[]{:T(128)}, bf16[8,64,256]{2,1,0:T(8,128)(2,1)S(1)}, s32[8]{0:T(128)S(1)}, ...), condition=%wide.region_1.2_spmd, body=%wide.region_0.1_spmd.sunk | while | flops 142819584 | bytes 592803 | solution.py:71
  147.6 4.3 fusion.49
  151.9 82.7 %while.27 = (s32[]{:T(128)}, f32[1,1024,1024]{2,1,0:T(8,128)}, bf16[1,8,2,1024,256]{4,3,2,1,0:T(8,128)(2,1)}, s32[1,8]{1,0:T(1,128)S(1)}, s32[8]{0:T(128)S(1)}, ...) while((s32[]{:T(128)}, f32[1,1024,1024]{2,1,0:T(8,128)}, ...), condition=%wide.region_19.20_spmd.clone, body=%wide.region_18.19_spmd.clone.sunk | while | flops 807862784 | bytes 12846747 | solution.py:63
  157.2 3.9 bitcast_add_fusion.3
  166.4 5.3 bitcast_add_fusion.3
  176.9 5.2 bitcast_add_fusion.3
  187.4 5.3 bitcast_add_fusion.3
  198.0 5.2 bitcast_add_fusion.3
  208.5 5.2 bitcast_add_fusion.3
  218.9 5.2 bitcast_add_fusion.3
  229.4 5.2 bitcast_add_fusion.3
  234.6 5.3 copy.37
  240.0 6.8 %fusion.36 = f32[1024,1024]{1,0:T(8,128)} fusion(f32[1,1024,1024]{1,2,0:T(8,128)} %copy.37, f32[1,1,1024,1024]{2,3,1,0:T(8,128)} %copy.34), kind=kLoop, calls=%fused_computation.53 | loop fusion | flops 1048576 | bytes 12582912 | tf_op jit(solution)/shard_map/transpose | solution.py:78
  246.8 5.5 copy.33
  252.3 4.4 fusion.26
  258.8 11.7 %cholesky.223 = f32[128,128]{1,0:T(8,128)S(1)} custom-call(f32[128,128]{1,0:T(8,128)S(1)} %cholesky.580), custom_call_target="Cholesky" | custom-call | tf_op jit(solution)/shard_map/jit(cholesky)/cholesky | solution.py:76
  270.5 9.8 %custom-call.63 = f32[1,128,128]{1,2,0:T(8,128)S(1)} custom-call(f32[1,128,128]{2,1,0:T(8,128)S(1)} %get-tuple-element.295), custom_call_target="InvertDiagBlocksLowerTriangular" | custom-call | tf_op jit(solution)/shard_map/jit(cholesky)/cholesky | solution.py:76
  280.3 2.5 cholesky.255
  282.8 2.4 constant_dynamic-update-slice_fusion.32
  286.8 11.9 %cholesky.244 = f32[128,128]{1,0:T(8,128)S(1)} custom-call(f32[128,128]{1,0:T(8,128)S(1)} %cholesky.584), custom_call_target="Cholesky" | custom-call | tf_op jit(solution)/shard_map/jit(cholesky)/cholesky | solution.py:76
  299.3 9.8 %custom-call.64 = f32[1,128,128]{1,2,0:T(8,128)S(1)} custom-call(f32[1,128,128]{2,1,0:T(8,128)S(1)} %get-tuple-element.292), custom_call_target="InvertDiagBlocksLowerTriangular" | custom-call | tf_op jit(solution)/shard_map/jit(cholesky)/cholesky | solution.py:76
  312.5 11.7 %cholesky.468 = f32[128,128]{1,0:T(8,128)S(1)} custom-call(f32[128,128]{1,0:T(8,128)S(1)} %cholesky.589), custom_call_target="Cholesky" | custom-call | tf_op jit(solution)/shard_map/jit(cholesky)/cholesky | solution.py:76
  325.5 9.8 %custom-call.65 = f32[1,128,128]{1,2,0:T(8,128)S(1)} custom-call(f32[1,128,128]{2,1,0:T(8,128)S(1)} %get-tuple-element.289), custom_call_target="InvertDiagBlocksLowerTriangular" | custom-call | tf_op jit(solution)/shard_map/jit(cholesky)/cholesky | solution.py:76
  336.5 2.4 convolution_subtract_fusion.7
  338.9 12.1 %cholesky.487 = f32[128,128]{1,0:T(8,128)S(1)} custom-call(f32[128,128]{1,0:T(8,128)S(1)} %cholesky.594), custom_call_target="Cholesky" | custom-call | tf_op jit(solution)/shard_map/jit(cholesky)/cholesky | solution.py:76
  352.3 9.8 %custom-call.66 = f32[1,128,128]{1,2,0:T(8,128)S(1)} custom-call(f32[1,128,128]{2,1,0:T(8,128)S(1)} %get-tuple-element.286), custom_call_target="InvertDiagBlocksLowerTriangular" | custom-call | tf_op jit(solution)/shard_map/jit(cholesky)/cholesky | solution.py:76
  363.2 2.3 convolution_subtract_fusion.8
  365.5 11.7 %cholesky.506 = f32[128,128]{1,0:T(8,128)S(1)} custom-call(f32[128,128]{1,0:T(8,128)S(1)} %cholesky.599), custom_call_target="Cholesky" | custom-call | tf_op jit(solution)/shard_map/jit(cholesky)/cholesky | solution.py:76
  378.5 9.9 %custom-call.67 = f32[1,128,128]{1,2,0:T(8,128)S(1)} custom-call(f32[1,128,128]{2,1,0:T(8,128)S(1)} %get-tuple-element.283), custom_call_target="InvertDiagBlocksLowerTriangular" | custom-call | tf_op jit(solution)/shard_map/jit(cholesky)/cholesky | solution.py:76
  391.8 11.7 %cholesky.526 = f32[128,128]{1,0:T(8,128)S(1)} custom-call(f32[128,128]{1,0:T(8,128)S(1)} %cholesky.604), custom_call_target="Cholesky" | custom-call | tf_op jit(solution)/shard_map/jit(cholesky)/cholesky | solution.py:76
  404.8 9.8 %custom-call.68 = f32[1,128,128]{1,2,0:T(8,128)S(1)} custom-call(f32[1,128,128]{2,1,0:T(8,128)S(1)} %get-tuple-element.280), custom_call_target="InvertDiagBlocksLowerTriangular" | custom-call | tf_op jit(solution)/shard_map/jit(cholesky)/cholesky | solution.py:76
  417.6 11.9 %cholesky.546 = f32[128,128]{1,0:T(8,128)S(1)} custom-call(f32[128,128]{1,0:T(8,128)S(1)} %cholesky.609), custom_call_target="Cholesky" | custom-call | tf_op jit(solution)/shard_map/jit(cholesky)/cholesky | solution.py:76
  430.7 9.8 %custom-call.69 = f32[1,128,128]{1,2,0:T(8,128)S(1)} custom-call(f32[1,128,128]{2,1,0:T(8,128)S(1)} %get-tuple-element.277), custom_call_target="InvertDiagBlocksLowerTriangular" | custom-call | tf_op jit(solution)/shard_map/jit(cholesky)/cholesky | solution.py:76
  443.2 11.7 %cholesky.564 = f32[128,128]{1,0:T(8,128)S(1)} custom-call(f32[128,128]{1,0:T(8,128)S(1)} %convolution_subtract_fusion.11), custom_call_target="Cholesky" | custom-call | tf_op jit(solution)/shard_map/jit(cholesky)/cholesky | solution.py:76
  461.8 6.7 %fusion.27 = (f32[1024,1024]{1,0:T(8,128)}, f32[1024,1024]{1,0:T(8,128)}) fusion(f32[1024,1024]{1,0:T(8,128)} %get-tuple-element.275, pred[]{:T(512)S(6)} %cholesky.579), kind=kLoop, calls=%fused_computation.44 | loop fusion | flops 4194304 | bytes 12582913 | tf_op jit(solution)/shard_map/jit(_solve_triangular)/triangular_solve | solution.py:78
  468.5 23.6 %while.26 = (s32[]{:T(128)}, f32[1024,1024]{1,0:T(8,128)}, s32[8,2]{0,1:T(2,128)S(1)}, f32[8,128,128]{2,1,0:T(8,128)S(1)}, s32[]{:T(128)}) while((s32[]{:T(128)}, f32[1024,1024]{1,0:T(8,128)}, s32[8,2]{0,1:T(2,128)S(1)}, f32[8,128,128]{2,1,0:T(8,128)S(1)}, s32[]{:T(128)}) %tuple.116), condition=%wide.while_cond, body=%wide.while_body.sunk | while | flops 2 | bytes 131189 | solution.py:78
  469.1 2.3 bitcast_dynamic-update-slice_fusion.3
  492.0 79.0 %custom-call.70 = f32[8,128,128]{1,2,0:T(8,128)S(1)} custom-call(f32[8,128,128]{2,1,0:T(8,128)S(1)} %get-tuple-element.167), custom_call_target="InvertDiagBlocksLowerTriangular" | custom-call | tf_op jit(solution)/shard_map/jit(_solve_triangular)/triangular_solve | solution.py:78
  583.5 2.6 convolution_subtract_fusion.2
  586.8 3.0 convolution_subtract_fusion.1
  590.4 3.7 convolution_subtract_fusion.3
  594.8 3.4 fusion.25
  598.2 5.4 copy.38
  (177 shorter events, 139.8 us)
Async XLA Ops:
  7.2 31.6 %copy-start = (s32[8,8]{1,0:T(8,128)S(1)}, s32[8,8]{1,0:T(8,128)}, u32[]{:S(2)}) copy-start(s32[8,8]{1,0:T(8,128)} %param.15) | copy-start | bytes 772
  7.2 87.9 %all-gather.9.cloned.1.call-start = ((), (), s32[]{:S(2)}) async-start(), calls=%async_computation.3 | async-start | bytes 8912896 | tf_op jit(solution)/shard_map/all_gather | solution.py:44
  23.4 128.6 %all-gather.7.cloned.1.call-start = ((), (), s32[]{:S(2)}) async-start(), calls=%async_computation.2 | async-start | bytes 9437184 | tf_op jit(solution)/shard_map/all_gather | solution.py:49
  24.1 222.7 %all-gather.5.cloned.1.call-start = ((), (), s32[]{:S(2)}) async-start(), calls=%async_computation.1 | async-start | bytes 4456448 | tf_op jit(solution)/shard_map/all_gather | solution.py:75
  100.8 46.8 %copy-start.7 = (f32[1,64,1024]{2,1,0:T(8,128)S(1)}, f32[1,64,1024]{2,1,0:T(8,128)}, u32[]{:S(2)}) copy-start(f32[1,64,1024]{2,1,0:T(8,128)} %param.11) | copy-start | bytes 786436
  256.8 2.0 copy-start.5
  571.0 4.3 copy-start.4
  586.8 8.0 %copy-start.3 = (f32[1,1024,1024]{1,2,0:T(8,128)S(1)}, f32[1,1024,1024]{1,2,0:T(8,128)}, u32[]{:S(2)}) copy-start(f32[1,1024,1024]{1,2,0:T(8,128)} %copy.37) | copy-start | bytes 12582916
  589.8 5.0 copy-start.2
  594.8 10.5 %copy-start.1 = (s32[8,8]{1,0:T(8,128)S(1)}, s32[8,8]{1,0:T(8,128)}, u32[]{:S(2)}) copy-start(s32[8,8]{1,0:T(8,128)} %param.15) | copy-start | bytes 772
  598.2 5.4 copy-start.6
Sparse Core Ops, SparseCore 0:
  23.5 71.5 all-gather.8
  96.8 49.8 all-gather.6
  152.0 50.9 all-gather.4
where the time goes:
time: 619 us; the launch traced here: 612 us
  other arithmetic  290 us (47%)
  matrix products  117 us (19%)
  local copies, waits for them, and re-layouts  89.3 us (14%)
  waiting for transfers between devices  57 us (9%)
  blocking collectives  21.8 us (4%)
  between operations  19.9 us (3%)
  loops' own time  17.2 us (3%)
    another operation x30, other arithmetic, shards(): factor = jnp.linalg.cholesky(whole_diag)  172 us
    another operation x3, other arithmetic, shards(): jax.scipy.linalg.solve_triangular(factor, stacked.T, lower=True)  85.7 us
    all_gather x1, waiting for transfers between devices, shards(): full_column = lax.all_gather(own_column, 'rows', axis=3, tiled=True)  56.3 us
    dot_general x8, matrix products, finish(): lax.dot_general(left_part, base_col, (((1,), (1,)), ((), ())), preferred_...  40.7 us
    another operation x15, matrix products, shards(): jax.scipy.linalg.solve_triangular(factor, stacked.T, lower=True)  23.6 us
    another operation x24, local copies, waits for them, and re-layouts  23.4 us
    another operation x14, matrix products, shards(): factor = jnp.linalg.cholesky(whole_diag)  23.1 us
    another operation x1, loops' own time, shards(): lax.map(diag_left, jnp.arange(base_full.shape[0], dtype=jnp.int32))  16.8 us
  transfers between devices with their start and end apart: 3, of which 1 were waited for; matrix products, arithmetic and copies ran while one was open for 23% of the time, Pallas kernels for 0%

commit v1 on v0

--- a/solution.py
+++ b/solution.py
@@ -1,7 +1,134 @@
 import jax
 import jax.numpy as jnp
 from jax import lax
+from jax.experimental import pallas as pl
+from jax.experimental.pallas import tpu as pltpu
 from jax.sharding import PartitionSpec as P
+
+NB = 128
+G = 8
+
+def split2(x):
+    hi = x.astype(jnp.bfloat16)
+    lo = (x - hi.astype(jnp.float32)).astype(jnp.bfloat16)
+    return hi, lo
+
+def nt(a, b):
+    return lax.dot_general(a, b, (((1,), (1,)), ((), ())), preferred_element_type=jnp.float32)
+
+def nt3(ah, al, bh, bl):
+    return nt(jnp.concatenate([ah, al, ah], axis=1), jnp.concatenate([bh, bh, bl], axis=1))
+
+def factor_block(t_ref):
+    for g in range(NB // G):
+        v = t_ref[g * G:(g + 1) * G, :]
+        cols = [jnp.broadcast_to(v[:, g * G + j:g * G + j + 1], (G, NB)) for j in range(G)]
+        b = [[jnp.broadcast_to(cols[j][s:s + 1, :], (G, NB)) if s >= j else None for j in range(G)] for s in range(G)]
+        low = [[None] * G for _ in range(G)]
+        rinv = [None] * G
+        r = [jnp.broadcast_to(v[s:s + 1, :], (G, 2 * NB)) for s in range(G)]
+        two = lambda x: jnp.concatenate([x, x], axis=1)
+        for j in range(G):
+            rinv[j] = lax.rsqrt(b[j][j])
+            for s in range(j + 1, G):
+                low[s][j] = b[s][j] * rinv[j]
+            for t in range(j + 1, G):
+                for s in range(t, G):
+                    b[s][t] = b[s][t] - low[s][j] * low[t][j]
+            r[j] = r[j] * two(rinv[j])
+            for s in range(j + 1, G):
+                r[s] = r[s] - two(low[s][j]) * r[j]
+        m = [None] * G
+        for s in reversed(range(G)):
+            acc = r[s]
+            for t in range(s + 1, G):
+                acc = acc - two(low[t][s]) * m[t]
+            m[s] = acc * two(rinv[s])
+        sub = lax.broadcasted_iota(jnp.int32, (G, 2 * NB), 0)
+        out = r[0]
+        for s in range(1, G):
+            out = jnp.where(sub == s, r[s], out)
+        t_ref[g * G:(g + 1) * G, :] = out
+        for rb in range(g + 1, NB // G):
+            w = t_ref[rb * G:(rb + 1) * G, :]
+            acc = w
+            for j in range(G):
+                wc = jnp.broadcast_to(w[:, g * G + j:g * G + j + 1], (G, NB))
+                acc = acc - two(wc) * m[j]
+            t_ref[rb * G:(rb + 1) * G, :] = acc
+
+def chol_body(a_ref, inv_ref, t_ref, ph_ref, pl_ref):
+    n = a_ref.shape[0]
+    nblk = n // NB
+    ri = lax.broadcasted_iota(jnp.int32, (NB, NB), 0)
+    ci = lax.broadcasted_iota(jnp.int32, (NB, NB), 1)
+
+    def step(j, _):
+        o = pl.multiple_of(j * NB, NB)
+        t_ref[:, :NB] = a_ref[pl.ds(o, NB), pl.ds(o, NB)]
+        t_ref[:, NB:] = jnp.where(ri == ci, 1.0, 0.0)
+        factor_block(t_ref)
+        inv = t_ref[:, NB:]
+        inv_ref[pl.ds(o, NB), :] = inv
+        low = jnp.where(ri >= ci, t_ref[:, :NB].T, 0.0)
+        ih, il = split2(inv)
+        for v in range(nblk // 2):
+            lo_row = 2 * NB * v
+            @pl.when((j + 1) // 2 == v)
+            def _():
+                p = a_ref[lo_row:, pl.ds(o, NB)]
+                ph, plo = split2(p)
+                x = nt3(ph, plo, ih, il)
+                rows = lax.broadcasted_iota(jnp.int32, x.shape, 0) + lo_row
+                x = jnp.where(rows >= o + NB, x, 0.0)
+                a_ref[lo_row:, pl.ds(o, NB)] = x
+                xh, xl = split2(x)
+                c = nt3(xh, xl, xh, xl)
+                a_ref[lo_row:, lo_row:] = a_ref[lo_row:, lo_row:] - c
+        a_ref[pl.ds(o, NB), pl.ds(o, NB)] = low
+        return 0
+    lax.fori_loop(0, nblk, step, 0)
+
+def solve_body(b_ref, l_ref, inv_ref, x_ref, xh_ref, xl_ref):
+    n = b_ref.shape[0]
+    for j in range(n // NB):
+        s = slice(j * NB, (j + 1) * NB)
+        ih, il = split2(inv_ref[s, :])
+        acc = b_ref[:, s]
+        if j:
+            lh, ll = split2(l_ref[s, :j * NB])
+            acc = acc - nt(xh_ref[:, :j * NB], lh) - nt(xl_ref[:, :j * NB], lh) - nt(xh_ref[:, :j * NB], ll)
+        ah, al = split2(acc)
+        x = nt3(ah, al, ih, il)
+        x_ref[:, s] = x
+        xh, xl = split2(x)
+        xh_ref[:, s] = xh
+        xl_ref[:, s] = xl
+
+def chol_kernel(d_ref, l_ref, inv_ref, t_ref):
+    n = l_ref.shape[0]
+    for i in range(n // NB):
+        si = slice(i * NB, (i + 1) * NB)
+        for j in range(i + 1):
+            sj = slice(j * NB, (j + 1) * NB)
+            l_ref[si, sj] = (d_ref[si, sj] + d_ref[sj, si].T) * 0.5
+    chol_body(l_ref, inv_ref, t_ref, None, None)
+    for j in range(n // NB):
+        if j + 1 < n // NB:
+            l_ref[j * NB:(j + 1) * NB, (j + 1) * NB:] = jnp.zeros((NB, n - (j + 1) * NB), jnp.float32)
+
+def chol(d):
+    n = d.shape[0]
+    return pl.pallas_call(chol_kernel,
+        out_shape=(jax.ShapeDtypeStruct((n, n), jnp.float32), jax.ShapeDtypeStruct((n, NB), jnp.float32)),
+        scratch_shapes=[pltpu.VMEM((NB, 2 * NB), jnp.float32)],
+        compiler_params=pltpu.CompilerParams(vmem_limit_bytes=60 << 20), name="chol")(d)
+
+def solve(b, l, inv):
+    n = b.shape[0]
+    return pl.pallas_call(solve_body, out_shape=jax.ShapeDtypeStruct(b.shape, jnp.float32),
+        scratch_shapes=[pltpu.VMEM((n, n), jnp.bfloat16)] * 2,
+        compiler_params=pltpu.CompilerParams(vmem_limit_bytes=60 << 20), name="solve")(b, l, inv)
 
 
 def core_of(side_row, rank_row, side_col, rank_col):
@@ -36,31 +163,23 @@
 def shards(band, diag, row_factors, row_ranks, col_factors, col_ranks):
     column = lax.axis_index("cols")
     slab_idx = lax.axis_index("rows")
-    row_count = row_factors.shape[0]
     slab_rows = diag.shape[1]
-    tile_order = band.shape[-1]
     own_ranks = lax.dynamic_index_in_dim(col_ranks, column, 0, keepdims=False)
     own_column = lax.all_to_all(col_factors, "cols", split_axis=0, concat_axis=1, tiled=True)
     full_column = lax.all_gather(own_column, "rows", axis=3, tiled=True)
     base_full = full_column[0, :, 0]
     side_full = full_column[0, :, 1]
     base_slab = own_column[0, :, 0]
-    start_sum = jnp.zeros((row_count, tile_order, tile_order), jnp.float32)
     factors = lax.all_gather(row_factors, "cols", axis=1, tiled=True)
     piece_ranks = lax.all_gather(row_ranks, "cols", axis=1, tiled=True)
 
-    def advance(inner, carried):
-        base_col = lax.dynamic_index_in_dim(base_full, inner, 0, keepdims=False)
-        side_col = lax.dynamic_index_in_dim(side_full, inner, 0, keepdims=False)
-        rank_col = lax.dynamic_index_in_dim(own_ranks, inner, 0, keepdims=False)
-        row_part = lax.dynamic_index_in_dim(factors, inner, 1, keepdims=False)
-        row_rank = lax.dynamic_index_in_dim(piece_ranks, inner, 1, keepdims=False)
-        tile_terms = [
-            pair_tile(row_part[0, 0], row_part[0, 1], row_rank[0], base_col, side_col, rank_col)
-        ]
-        return carried + jnp.stack(tile_terms)
-
-    update = lax.fori_loop(0, factors.shape[1], advance, start_sum)
+    row_pos = jnp.arange(factors.shape[-1], dtype=jnp.int32)
+    rows0 = factors[0]
+    core = jnp.einsum("kxa,kxb->kab", rows0[:, 1], side_full, preferred_element_type=jnp.float32)
+    kept = (row_pos[None, :, None] < piece_ranks[0][:, None, None]) & (row_pos[None, None, :] < own_ranks[:, None, None])
+    core = jnp.where(kept, core, 0.0).astype(jnp.bfloat16)
+    left = jnp.einsum("kxa,kab->kxb", rows0[:, 0], core, preferred_element_type=jnp.float32).astype(jnp.bfloat16)
+    update = jnp.einsum("kxb,kyb->xy", left, base_full, preferred_element_type=jnp.float32)[None]
 
     def diag_left(panel_idx):
         side_col = lax.dynamic_index_in_dim(side_full, panel_idx, 0, keepdims=False)
@@ -73,11 +192,8 @@
     updated = band[:, 0] - update
     new_slab = diag[0] - diag_term
     whole_diag = lax.all_gather(new_slab, "rows", axis=0, tiled=True)
-    factor = jnp.linalg.cholesky(whole_diag)
-    stacked = updated.reshape(row_count * tile_order, tile_order)
-    solved = jax.scipy.linalg.solve_triangular(factor, stacked.T, lower=True).T.reshape(
-        row_count, tile_order, tile_order
-    )
+    factor, inverses = chol(whole_diag)
+    solved = solve(updated[0], factor, inverses)[None]
     is_first = column == 0
     band_out = jnp.where(is_first, solved, updated)[:, None]
     factor_slab = lax.dynamic_slice_in_dim(factor, slab_idx * slab_rows, slab_rows, 0)

time: 619 us -> 285 us (0.46)
  other arithmetic: 290 us -> 12.5 us
  matrix products: 117 us -> 35.6 us
  local copies, waits for them, and re-layouts: 89.3 us -> 17 us
  Pallas kernels: 0 us -> 69.7 us
  waiting for transfers between devices: 57 us -> 96 us
    another operation x33 -> x0, other arithmetic: 258 us -> none  [the longest x30 172 us: shards(): factor = jnp.linalg.cholesky(whole_diag)]
    pallas_call x0 -> x2, Pallas kernels: none -> 69.7 us  [the longest x1 54.9 us: chol(): pl.pallas_call(chol_kernel, out_shape=(jax.ShapeDtypeStruct((n, n), jnp.f...]
    another operation x29 -> x0, matrix products: 46.7 us -> none  [the longest x15 23.6 us: shards(): jax.scipy.linalg.solve_triangular(factor, stacked.T, lower=True)]
    dot_general x16 -> x2, matrix products: 51.8 us -> 17.4 us  [the longest x1 12.4 us: shards(): jnp.einsum('kxb,kyb->xy', left, base_full, preferred_element_type=jnp.flo...]
    another operation x33 -> x0, local copies, waits for them, and re-layouts: 25.9 us -> none
    all_gather x1, waiting for transfers between devices: 0.01 us -> 24.5 us  [shards(): whole_diag = lax.all_gather(new_slab, 'rows', axis=0, tiled=True)]
    all_gather x1, waiting for transfers between devices: 56.3 us -> 70.8 us  [shards(): full_column = lax.all_gather(own_column, 'rows', axis=3, tiled=True)]
    unnamed x21 -> x11, local copies, waits for them, and re-layouts: 14.8 us -> 1.28 us
  transfers between devices with their start and end apart: 3 -> 3, of which waited for: 1 -> 2; matrix products, arithmetic and copies ran while one was open for 23% -> 20% of each run, Pallas kernels for 0% -> 0%
where the time goes in v1:
time: 285 us; the launch traced here: 284 us
  waiting for transfers between devices  96 us (34%)
  Pallas kernels  69.7 us (24%)
  matrix products  35.6 us (12%)
  blocking collectives  23 us (8%)
  local copies, waits for them, and re-layouts  17 us (6%)
  loops' own time  15.4 us (5%)
  between operations  14.5 us (5%)
  other arithmetic  12.5 us (4%)
    all_gather x1, waiting for transfers between devices, shards(): full_column = lax.all_gather(own_column, 'rows', axis=3, tiled=True)  70.8 us
    pallas_call x1, Pallas kernels, chol(): pl.pallas_call(chol_kernel, out_shape=(jax.ShapeDtypeStruct((n, n), jnp.f...  54.9 us
    all_gather x1, waiting for transfers between devices, shards(): whole_diag = lax.all_gather(new_slab, 'rows', axis=0, tiled=True)  24.5 us
    another operation x1, loops' own time, shards(): lax.map(diag_left, jnp.arange(base_full.shape[0], dtype=jnp.int32))  15.4 us
    all_to_all x1, blocking collectives, shards(): lax.all_to_all(col_factors, 'cols', split_axis=0, concat_axis=1, tiled=True)  15.3 us
    pallas_call x1, Pallas kernels, solve(): pl.pallas_call(solve_body, out_shape=jax.ShapeDtypeStruct(b.shape, jnp.fl...  14.8 us
    dot_general x8, matrix products, weighted(): jnp.dot(base_row, pair_core, preferred_element_type=jnp.float32)  13.8 us
    dot_general x1, matrix products, shards(): jnp.einsum('kxb,kyb->xy', left, base_full, preferred_element_type=jnp.flo...  12.4 us
  transfers between devices with their start and end apart: 3, of which 2 were waited for; matrix products, arithmetic and copies ran while one was open for 20% of the time, Pallas kernels for 0%

profile of v1, /device:TPU:1, one launch (start us, length us, event | category | flops | bytes accessed | tf_op | source)
XLA Modules:
  0.0 283.9 jit_solution(4334909480717034234)
XLA Ops:
  7.2 15.3 %all_to_all.12 = bf16[8,1,2,64,256]{4,3,2,1,0:T(8,128)(2,1)S(1)} all-to-all(bf16[8,1,2,64,256]{4,3,2,1,0:T(8,128)(2,1)} %param.12), channel_id=1, replica_groups=mesh['rows'=16,'cols'=8] {'cols'}, dimensions={0} | all-to-all | bytes 1048576 | tf_op jit(solution)/shard_map/all_to_all | solution.py:168
  22.5 0.8 copy.10
  23.4 0.7 all-gather.5.cloned.1.call-update
  24.2 70.8 %all-gather.9.cloned.1.call-done = bf16[8,1,2,1024,256]{4,3,0,2,1:T(8,128)(2,1)} async-done(((bf16[8,1,2,64,256]{4,3,0,2,1:T(8,128)(2,1)}), bf16[8,1,2,1024,256]{4,3,0,2,1:T(8,128)(2,1)}) %all-gather.9.cloned.1.call-update) | async-done | bytes 8388624 | tf_op jit(solution)/shard_map/all_gather | solution.py:169
  95.0 4.5 %slice_bitcast_fusion.1 = bf16[8,1024,256]{2,1,0:T(8,128)(2,1)} fusion(bf16[1,8,2,1024,256]{4,3,1,2,0:T(8,128)(2,1)} %bitcast.83), kind=kLoop, calls=%fused_computation.18 | loop fusion | bytes 8388608 | tf_op jit(solution)/shard_map/squeeze | solution.py:171
  99.5 44.8 %while.10 = (s32[]{:T(128)}, bf16[8,64,256]{2,1,0:T(8,128)(2,1)S(1)}, s32[8]{0:T(128)S(1)}, bf16[8,64,256]{2,1,0:T(8,128)(2,1)S(1)}, s32[8]{0:T(128)S(1)}, /*ind...) while((s32[]{:T(128)}, bf16[8,64,256]{2,1,0:T(8,128)(2,1)S(1)}, s32[8]{0:T(128)S(1)}, ...), condition=%wide.region_1.2_spmd, body=%wide.region_0.1_spmd.sunk | while | flops 142819584 | bytes 592795 | solution.py:190
  99.5 0.6 dynamic_slice.42
  102.0 0.7 dynamic_slice.43
  102.7 0.6 iota_compare_fusion.4
  103.3 1.8 fusion.35
  105.1 0.7 dynamic_slice.42
  107.7 0.7 dynamic_slice.43
  108.3 0.6 iota_compare_fusion.4
  109.0 1.7 fusion.35
  110.7 0.7 dynamic_slice.42
  113.3 0.7 dynamic_slice.43
  113.9 0.6 iota_compare_fusion.4
  114.6 1.7 fusion.35
  116.3 0.7 dynamic_slice.42
  118.8 0.7 dynamic_slice.43
  119.5 0.6 iota_compare_fusion.4
  120.1 1.7 fusion.35
  121.9 0.7 dynamic_slice.42
  124.4 0.7 dynamic_slice.43
  125.1 0.6 iota_compare_fusion.4
  125.7 1.8 fusion.35
  127.5 0.7 dynamic_slice.42
  130.0 0.7 dynamic_slice.43
  130.7 0.6 iota_compare_fusion.4
  131.3 1.7 fusion.35
  133.1 0.7 dynamic_slice.42
  135.6 0.7 dynamic_slice.43
  136.3 0.6 iota_compare_fusion.4
  136.9 1.7 fusion.35
  138.6 0.7 dynamic_slice.42
  141.2 0.7 dynamic_slice.43
  141.8 0.6 iota_compare_fusion.4
  142.5 1.8 fusion.35
  144.3 4.4 %fusion.27 = f32[64,1024]{1,0:T(8,128)} fusion(bf16[8,64,256]{2,1,0:T(8,128)(2,1)S(1)} %get-tuple-element.36, bf16[1,8,2,1024,256]{4,3,1,2,0:T(8,128)(2,1)} %bitcast.84, f32[1,64,1024]{2,1,0:T(8,128)S(1)} %copy-done.2), kind=kOutput, calls=%fused_computation.31 | convolution fusion | flops 268500992 | bytes 4980736 | tf_op jit(solution)/shard_map/kxr,kyr->xy/dot_general | solution.py:191
  149.9 0.7 bitcast_dynamic-update-slice_fusion
  150.6 7.7 %all-reduce = s32[8]{0:T(128)S(1)} all-reduce(s32[8]{0:T(128)S(1)} %bitcast_dynamic-update-slice_fusion), channel_id=1, replica_groups=mesh['rows'=16,'cols'=8] {'cols'}, use_global_device_ids=true, to_apply=%add | all-reduce | flops 8 | bytes 64
  158.4 5.1 %select_convert_fusion = bf16[8,256,256]{2,1,0:T(8,128)(2,1)S(1)} fusion(bf16[8,2,1024,256]{3,2,1,0:T(8,128)(2,1)} %bitcast.88, pred[8,256]{1,0:T(8,128)(4,1)S(1)} %iota_compare_fusion.1, pred[8,256]{1,0:T(8,128)(4,1)S(1)} %iota_compare_fusion.2, bf16[1,8,2,1024,256]{4,3,1,2,0:T(8,128)(2,1)} %bitcast.85), kind=kOutput, calls=%fused_computation.29 | convolution fusion | flops 1075314688 | bytes 9441280 | tf_op jit(solution)/shard_map/kxa,kxb->kab/dot_general | solution.py:178
  163.5 12.4 %bitcast_subtract_fusion.b_ref = f32[1024,1024]{1,0:T(8,128)} fusion(f32[1,1,1024,1024]{3,2,1,0:T(8,128)} %param.8, bf16[1,8,2,1024,256]{4,3,1,2,0:T(8,128)(2,1)} %bitcast.86, bf16[8,256,256]{2,1,0:T(8,128)(2,1)S(1)} %select_convert_fusion, bf16[8,2,1024,256]{3,2,1,0:T(8,128)(2,1)} %bitcast.89), kind=kOutput, calls=%fused_computation.23 | convolution fusion | flops 5371854848 | bytes 17825792 | tf_op jit(solution)/shard_map/kxb,kyb->xy/dot_general | solution.py:182
  175.9 24.5 %all-gather.7.cloned.1.call-done.d_ref = f32[1024,1024]{1,0:T(8,128)} async-done(((f32[64,1024]{1,0:T(8,128)}), f32[1024,1024]{1,0:T(8,128)}) %all-gather.7.cloned.1.call-update) | async-done | bytes 4194320 | tf_op jit(solution)/shard_map/all_gather | solution.py:194
  200.4 54.9 %chol.1 = (f32[1024,1024]{1,0:T(8,128)}, f32[1024,128]{1,0:T(8,128)}) custom-call(f32[1024,1024]{1,0:T(8,128)} %all-gather.7.cloned.1.call-done.d_ref), custom_call_target="tpu_custom_call" | custom-call | tf_op jit(solution)/shard_map/chol/pallas_call | solution.py:122
  255.3 14.8 %solve.1 = f32[1024,1024]{1,0:T(8,128)} custom-call(f32[1024,1024]{1,0:T(8,128)} %bitcast_subtract_fusion.b_ref, f32[1024,1024]{1,0:T(8,128)} %get-tuple-element.37.l_ref, f32[1024,128]{1,0:T(8,128)} %get-tuple-element.38.inv_ref), custom_call_target="tpu_custom_call" | custom-call | tf_op jit(solution)/shard_map/solve/pallas_call | solution.py:129
  270.1 5.6 %select_bitcast_fusion = f32[1,1,1024,1024]{3,2,1,0:T(8,128)} fusion(f32[1024,1024]{1,0:T(8,128)} %solve.1, f32[1024,1024]{1,0:T(8,128)} %bitcast_subtract_fusion.b_ref, pred[]{:T(512)S(6)} %eq.3), kind=kLoop, calls=%fused_computation.26 | loop fusion | flops 1048576 | bytes 12582913 | tf_op jit(solution)/shard_map/broadcast_in_dim | solution.py:198
  275.7 1.7 select_bitcast_fusion.1
  (22 shorter events, 0.9 us)
Async XLA Ops:
  7.2 17.0 %copy-start = (s32[8,8]{1,0:T(8,128)S(1)}, s32[8,8]{1,0:T(8,128)}, u32[]{:S(2)}) copy-start(s32[8,8]{1,0:T(8,128)} %param.13) | copy-start | bytes 772
  7.2 87.8 %all-gather.9.cloned.1.call-start = ((), (), s32[]{:S(2)}) async-start(), calls=%async_computation.3 | async-start | bytes 8912896 | tf_op jit(solution)/shard_map/all_gather | solution.py:169
  23.4 135.1 %all-gather.5.cloned.1.call-start = ((), (), s32[]{:S(2)}) async-start(), calls=%async_computation.1 | async-start | bytes 9437184 | tf_op jit(solution)/shard_map/all_gather | solution.py:173
  24.1 176.3 %all-gather.7.cloned.1.call-start = ((), (), s32[]{:S(2)}) async-start(), calls=%async_computation.2 | async-start | bytes 4456448 | tf_op jit(solution)/shard_map/all_gather | solution.py:194
  99.5 44.8 %copy-start.2 = (f32[1,64,1024]{2,1,0:T(8,128)S(1)}, f32[1,64,1024]{2,1,0:T(8,128)}, u32[]{:S(2)}) copy-start(f32[1,64,1024]{2,1,0:T(8,128)} %param.9) | copy-start | bytes 786436
  144.3 5.1 %copy-start.3 = (u32[128]{0:T(128)S(1)}, u32[128]{0:T(128)}, u32[]{:S(2)}) copy-start(u32[128]{0:T(128)} %constant.53) | copy-start | bytes 1540
  270.1 5.6 %copy-start.1 = (f32[64,1024]{1,0:T(8,128)S(1)}, f32[64,1024]{1,0:T(8,128)}, u32[]{:S(2)}) copy-start(f32[64,1024]{1,0:T(8,128)} %fusion.27) | copy-start | bytes 786436
Sparse Core Ops, SparseCore 0:
  23.5 71.4 all-gather.8
  96.7 49.8 all-gather.4
  149.3 51.0 all-gather.6
